TPU v7x, 32 devices: a whole 2x2x4 slice. The times are simulated.
32 devices in a mesh: seg: 8 (over z, x), rep: 4 (over y, core).
Axes of the slice: x: 2, y: 2, z: 4, core: 2. Of those that a mesh axis runs over, the one named last changes fastest.
Arguments:
- decoder_rows: bfloat16 [256, 4096], P('rep', 'seg'), may hold values from -2000 to 2000
- norm_gain: float32 [4096], replicated, may hold values from 0.5 to 1.5
- query_weight: bfloat16 [4096, 4096], P('rep', 'seg'), may hold values from -1 to 1
- key_codes: bfloat16 [4, 4096, 4096], P('rep', 'seg'), may hold values from -127 to 127, as said below
- key_scale: float32 [4, 32, 64], P('rep', 'seg'), may hold values from 0.5 to 1.5
- value_codes: bfloat16 [4, 4096, 4096], P('rep', 'seg'), may hold values from -6 to 6
- value_scale: float32 [4, 32, 64], P('rep', 'seg'), may hold values from 0.5 to 2
- enc_lengths: int32 [4], P('rep'), may hold values from 1024 to 4096
- output_weight: bfloat16 [4096, 4096], P('seg', 'rep'), may hold values from -0.09375 to 0.09375
Outputs:
- update: bfloat16 [256, 4096], P('rep', 'seg')
Inputs may be any that keep to these rules, and one draw needn't show every extreme that they name: `key_codes`: codes of a block times its scale give the cached keys.
All inputs are finite; a program needn't handle non-finite values.
Results may differ from a plain program's by a relative error of at most 0.011.
Values may be sent and summed in bfloat16 or wider, within the bound.
A program may use at most 64 MiB of HBM per device.

v0:
```python
import jax
import jax.numpy as jnp
from jax import lax
from jax.sharding import PartitionSpec as P


def per_device(
    decoder_rows,
    norm_gain,
    query_weight,
    key_codes,
    key_scale,
    value_codes,
    value_scale,
    enc_lengths,
    output_weight,
):
    gathered = lax.all_gather(decoder_rows, "seg", axis=1, tiled=True)
    widened = gathered.astype(jnp.float32)
    variance = jnp.mean(widened * widened, axis=-1, keepdims=True)
    normed = (widened * lax.rsqrt(variance + 1e-06) * norm_gain[None, :]).astype(jnp.bfloat16)
    query_own = jnp.dot(
        normed,
        lax.all_gather(query_weight, "rep", axis=0, tiled=True),
        preferred_element_type=jnp.float32,
    ).astype(jnp.bfloat16)
    queries = lax.all_gather(query_own, "seg", axis=1, tiled=True)
    docs_here, seg_length, inner_width = key_codes.shape
    head_count = key_scale.shape[2]
    head_dim = inner_width // head_count
    block_length = seg_length // key_scale.shape[1]
    per_doc = queries.shape[0] // docs_here
    row_count = docs_here * per_doc
    first_pos = lax.axis_index("seg") * seg_length
    positions = first_pos + jnp.arange(seg_length, dtype=jnp.int32)

    def one_doc(group_members):
        (
            document_query,
            document_keys,
            document_values,
            document_key_scale,
            document_value_scale,
            document_length,
        ) = group_members
        split_query = document_query.reshape(per_doc, head_count, head_dim)
        split_keys = document_keys.reshape(seg_length, head_count, head_dim)
        split_values = document_values.reshape(seg_length, head_count, head_dim)
        attention_scores = jnp.einsum(
            "qhd,khd->qhk", split_query, split_keys, preferred_element_type=jnp.float32
        )
        key_multiplier = jnp.repeat(document_key_scale, block_length, axis=0).T
        value_factor = jnp.repeat(document_value_scale, block_length, axis=0).T
        attention_scores = attention_scores * key_multiplier[None]
        usable = (positions < document_length)[None, None, :]
        attention_scores = jnp.where(usable, attention_scores, jnp.float32(-1e30))
        peaks = jnp.max(attention_scores, axis=-1)
        weights = jnp.where(usable, jnp.exp(attention_scores - peaks[..., None]), jnp.float32(0.0))
        totals = jnp.sum(weights, axis=-1)
        scaled = (weights * value_factor[None]).astype(jnp.bfloat16)
        attended = jnp.einsum(
            "qhk,khd->qhd", scaled, split_values, preferred_element_type=jnp.float32
        )
        return (peaks, totals, attended.reshape(per_doc, inner_width))

    query_docs = queries.reshape(docs_here, per_doc, inner_width)
    peaks, totals, outputs = lax.map(
        one_doc, (query_docs, key_codes, value_codes, key_scale, value_scale, enc_lengths)
    )
    peaks = peaks.reshape(row_count, head_count)
    totals = totals.reshape(row_count, head_count)
    outputs = outputs.reshape(row_count, inner_width)
    seg_count = lax.axis_size("seg")
    own_heads = head_count // seg_count
    received = (
        lax.all_to_all(peaks[None], "seg", split_axis=2, concat_axis=0, tiled=True),
        lax.all_to_all(totals[None], "seg", split_axis=2, concat_axis=0, tiled=True),
        lax.all_to_all(outputs[None], "seg", split_axis=2, concat_axis=0, tiled=True),
    )
    peak_all, total_all, out_all = received
    largest = jnp.max(peak_all, axis=0)
    factor = jnp.exp(peak_all - largest[None])
    denominator = jnp.sum(factor * total_all, axis=0)
    numerator = jnp.sum(
        out_all.reshape(seg_count, row_count, own_heads, head_dim) * factor[..., None], axis=0
    )
    attn_own = (
        (numerator / denominator[..., None])
        .reshape(row_count, own_heads * head_dim)
        .astype(jnp.bfloat16)
    )
    partial_terms = jnp.dot(
        attn_own,
        lax.all_gather(output_weight, "rep", axis=1, tiled=True),
        preferred_element_type=jnp.float32,
    )
    return lax.psum_scatter(partial_terms, "seg", scatter_dimension=1, tiled=True).astype(
        jnp.bfloat16
    )


def solution(mesh):
    placed = (
        P("rep", "seg"),
        P(),
        P("rep", "seg"),
        P("rep", "seg", None),
        P("rep", "seg", None),
        P("rep", "seg", None),
        P("rep", "seg", None),
        P("rep"),
        P("seg", "rep"),
    )
    return jax.shard_map(
        per_device, mesh=mesh, in_specs=placed, out_specs=P("rep", "seg"), check_vma=False
    )
```

profile of v0, /device:TPU:0, one launch (start us, length us, event | category | flops | bytes accessed | tf_op | source)
XLA Modules:
  0.0 250.8 jit_solution(3098906229739473497)
XLA Ops:
  6.5 0.0 all-gather.3.cloned.1.call-start
  6.5 0.7 all-gather.3.cloned.1.call-update
  7.3 0.0 all-gather.5.cloned.1.call-start
  7.3 0.7 all-gather.5.cloned.1.call-update
  8.0 0.8 copy.36
  8.8 0.1 broadcast_in_dim.60
  9.6 0.0 copy-start.1
  9.6 0.0 copy-start.2
  9.6 6.6 %copy.34 = bf16[1,512,4096]{1,2,0:T(8,128)(2,1)} copy(bf16[1,512,4096]{2,1,0:T(8,128)(2,1)} %param.12) | data formatting | bytes 8388608 | tf_op args[3]
  16.2 0.0 copy-done.1
  16.2 33.2 %all_gather.12 = bf16[64,4096]{1,0:T(8,128)(2,1)S(1)} all-gather(bf16[64,512]{1,0:T(8,128)(2,1)S(1)} %copy-done.1), channel_id=1, replica_groups=mesh['seg'=8,'rep'=4] {'seg'}, dimensions={1}, use_global_device_ids=true | all-gather | bytes 589824 | tf_op jit(solution)/shard_map/all_gather | solution.py:18
  49.3 0.2 fusion.13
  49.6 0.0 all-gather.3.cloned.1.call-done
  49.6 0.0 copy-done.2
  49.6 3.1 %convolution_convert_fusion = bf16[64,512]{1,0:T(8,128)(2,1)S(1)} fusion(bf16[4096,512]{1,0:T(8,128)(2,1)} %all-gather.3.cloned.1.call-done, bf16[64,4096]{1,0:T(8,128)(2,1)S(1)} %all_gather.12, f32[4096]{0:T(1024)S(1)} %copy-done.2, f32[64]{0:T(128)S(1)} %add_rsqrt_fusion), kind=kOutput, calls=%fused_computation.20 | convolution fusion | flops 269516800 | bytes 4800768 | tf_op jit(solution)/shard_map/dot_general | solution.py:22
  52.7 31.6 %all_gather.14 = bf16[64,4096]{1,0:T(8,128)(2,1)S(1)} all-gather(bf16[64,512]{1,0:T(8,128)(2,1)S(1)} %convolution_convert_fusion), channel_id=1, replica_groups=mesh['seg'=8,'rep'=4] {'seg'}, dimensions={1}, use_global_device_ids=true | all-gather | bytes 589824 | tf_op jit(solution)/shard_map/all_gather | solution.py:27
  84.3 1.1 reshape.64
  85.4 4.2 %bitcast_reduce_fusion = (f32[64,64]{0,1:T(8,128)S(1)}, f32[64,64,512]{2,1,0:T(8,128)S(1)}) fusion(f32[64,512]{1,0:T(8,128)S(1)} %bitcast.79, pred[512]{0:T(512)(128)(4,1)S(1)} %add_compare_fusion, bf16[512,64,64]{0,2,1:T(8,128)(2,1)} %bitcast.75, bf16[64,64,64]{2,1,0:T(8,128)(2,1)S(1)} %reshape.64), kind=kOutput, calls=%fused_computation.1 | convolution fusion | flops 274722816 | bytes 13255168 | tf_op jit(solution)/shard_map/while/body/eval_jaxpr/qhd,khd->qhk/dot_general | solution.py:49
  89.6 0.0 copy-start
  89.6 2.8 %fusion.2 = f32[64,64]{0,1:T(8,128)S(1)} fusion(f32[64,64,512]{2,1,0:T(8,128)S(1)} %get-tuple-element.28, f32[64,64]{0,1:T(8,128)S(1)} %get-tuple-element.27, f32[64,512]{1,0:T(8,128)S(1)} %bitcast.80, pred[512]{0:T(512)(128)(4,1)S(1)} %add_compare_fusion), kind=kLoop, calls=%fused_computation.6 | loop fusion | flops 10481664 | bytes 8552960 | tf_op jit(solution)/shard_map/while/body/eval_jaxpr/reduce_sum | solution.py:59
  92.4 0.4 copy-done
  92.8 0.5 broadcast.37
  93.3 0.7 reduce.4
  94.0 0.7 reshape.73
  94.7 5.3 %all-to-all-start.2 = ((f32[8,1,512]{2,1,0:T(1,128)}), f32[8,1,512]{2,1,0:T(1,128)S(1)}, u32[]{:S(2)}, u32[]{:S(2)}) async-start(f32[8,1,512]{2,1,0:T(1,128)} %reshape.73), calls=%async_computation.2 | async-start | bytes 32768 | tf_op jit(solution)/shard_map/all_to_all | solution.py:77
  100.1 0.0 copy-start.3
  100.1 6.5 %copy.39 = bf16[1,512,4096]{1,2,0:T(8,128)(2,1)} copy(bf16[1,512,4096]{2,1,0:T(8,128)(2,1)} %param.14) | data formatting | bytes 8388608 | tf_op args[5]
  106.5 0.0 copy-done.3
  106.6 0.1 copy.38
  106.6 0.1 broadcast_in_dim.63
  106.8 0.7 reduce.6
  107.5 0.7 reshape.71
  108.2 0.0 all-to-all-done.2
  108.2 6.0 %all-to-all-start.1 = ((f32[8,1,512]{2,1,0:T(1,128)}), f32[8,1,512]{2,1,0:T(1,128)S(1)}, u32[]{:S(2)}, u32[]{:S(2)}) async-start(f32[8,1,512]{2,1,0:T(1,128)} %reshape.71), calls=%async_computation.1 | async-start | bytes 32768 | tf_op jit(solution)/shard_map/all_to_all | solution.py:76
  114.2 8.5 %fusion.12 = f32[64,64,64]{2,0,1:T(8,128)} fusion(bf16[512,64,64]{0,2,1:T(8,128)(2,1)} %bitcast.78, f32[64,64,512]{2,1,0:T(8,128)} %copy-done, f32[64,512]{1,0:T(8,128)S(1)} %bitcast.88, f32[64,64]{0,1:T(8,128)S(1)} %get-tuple-element.27, f32[64,512]{1,0:T(8,128)S(1)} %bitcast.81, pred[512]{0:T(512)(128)(4,1)S(1)} %add_compare_fusion), kind=kOutput, calls=%fused_computation.17 | convolution fusion | flops 281018368 | bytes 13910528 | tf_op jit(solution)/shard_map/while/body/eval_jaxpr/qhk,khd->qhd/dot_general | solution.py:61
  122.7 1.9 copy.42
  124.6 19.3 %reduce.2 = f32[4096,64]{1,0:T(8,128)} reduce(f32[4096,1,64]{2,1,0:T(1,128)S(1)} %bitcast.77, f32[]{:T(128)} %broadcast.37), dimensions={1}, to_apply=%bitcast.59.reduce_sub_computation | reduce | bytes 2097156
  144.0 3.4 %reshape.69 = f32[8,1,32768]{2,1,0:T(1,128)} reshape(f32[4096,64]{1,0:T(8,128)} %reduce.2) | data formatting | bytes 2097152
  147.3 0.0 all-to-all-done.1
  147.3 6.0 %all-to-all-start = ((f32[8,1,32768]{2,1,0:T(1,128)}), f32[8,1,32768]{2,1,0:T(1,128)S(1)}, u32[]{:S(2)}, u32[]{:S(2)}) async-start(f32[8,1,32768]{2,1,0:T(1,128)} %reshape.69), calls=%async_computation | async-start | bytes 2097152 | tf_op jit(solution)/shard_map/all_to_all | solution.py:78
  153.3 0.3 reduce-scatter.2.cloned.1.call-start
  153.6 0.7 reduce.5
  154.3 0.1 reshape.74
  154.4 0.7 reduce.7
  155.0 0.1 reshape.72
  155.1 14.8 %all-to-all-done = f32[8,1,32768]{2,1,0:T(1,128)S(1)} async-done(((f32[8,1,32768]{2,1,0:T(1,128)}), f32[8,1,32768]{2,1,0:T(1,128)S(1)}, u32[]{:S(2)}, u32[]{:S(2)}) %all-to-all-start) | async-done | bytes 1048608 | tf_op jit(solution)/shard_map/all_to_all | solution.py:78
  169.9 3.1 %reduce.3 = f32[8,32768]{1,0:T(8,128)S(1)} reduce(f32[8,1,32768]{2,1,0:T(1,128)S(1)} %all-to-all-done, f32[]{:T(128)} %broadcast.37), dimensions={1}, to_apply=%all_to_all.37.reduce_sub_computation | reduce | bytes 2097156 | tf_op jit(solution)/shard_map/all_to_all | solution.py:78
  173.0 2.6 %reshape.70 = f32[4096,1,64]{2,1,0:T(1,128)S(1)} reshape(f32[8,32768]{1,0:T(8,128)S(1)} %reduce.3) | data formatting | bytes 2097152
  175.7 0.2 fusion.11
  175.9 0.0 all-gather.5.cloned.1.call-done
  176.0 4.0 %fusion.24 = f32[64,4096]{1,0:T(8,128)} fusion(bf16[64,512]{0,1:T(8,128)(2,1)S(1)} %fusion.21, bf16[512,4096]{1,0:T(8,128)(2,1)} %all-gather.5.cloned.1.call-done), kind=kOutput, calls=%fused_computation.38 | convolution fusion | flops 268435456 | bytes 5308416 | tf_op jit(solution)/shard_map/dot_general | solution.py:92
  180.0 0.0 reduce-scatter.2.cloned.1.call-update
  180.0 62.7 %reduce-scatter.2.cloned.1.call-done = f32[64,512]{1,0:T(8,128)} async-done(((f32[64,4096]{1,0:T(8,128)}), f32[64,512]{1,0:T(8,128)}) %reduce-scatter.2.cloned.1.call-update) | async-done | bytes 131088 | tf_op jit(solution)/shard_map/reduce_scatter | solution.py:97
  242.7 1.5 convert_element_type.24
  (7 shorter events, 0.1 us)
Async XLA Ops:
  6.5 43.0 %all-gather.3.cloned.1.call-start = ((), (), s32[]{:S(2)}) async-start(), calls=%async_computation.4 | async-start | bytes 5242880 | tf_op jit(solution)/shard_map/all_gather | solution.py:24
  7.3 168.7 %all-gather.5.cloned.1.call-start = ((), (), s32[]{:S(2)}) async-start(), calls=%async_computation.5 | async-start | bytes 5242880 | tf_op jit(solution)/shard_map/all_gather | solution.py:94
  9.6 6.6 %copy-start.1 = (bf16[64,512]{1,0:T(8,128)(2,1)S(1)}, bf16[64,512]{1,0:T(8,128)(2,1)}, u32[]{:S(2)}) copy-start(bf16[64,512]{1,0:T(8,128)(2,1)} %param.9) | copy-start | bytes 196612
  9.6 40.0 %copy-start.2 = (f32[4096]{0:T(1024)S(1)}, f32[4096]{0:T(1024)}, u32[]{:S(2)}) copy-start(f32[4096]{0:T(1024)} %param.10) | copy-start | bytes 49156
  89.6 3.2 %copy-start = (f32[64,64,512]{2,1,0:T(8,128)}, f32[64,64,512]{2,1,0:T(8,128)S(1)}, u32[]{:S(2)}) copy-start(f32[64,64,512]{2,1,0:T(8,128)S(1)} %get-tuple-element.28) | copy-start | bytes 25165828
  94.7 13.5 %all-to-all-start.2 = ((f32[8,1,512]{2,1,0:T(1,128)}), f32[8,1,512]{2,1,0:T(1,128)S(1)}, u32[]{:S(2)}, u32[]{:S(2)}) async-start(f32[8,1,512]{2,1,0:T(1,128)} %reshape.73), calls=%async_computation.2 | async-start | bytes 32768 | tf_op jit(solution)/shard_map/all_to_all | solution.py:77
  100.1 6.5 %copy-start.3 = (f32[1,4,64]{2,1,0:T(4,128)S(1)}, f32[1,4,64]{2,1,0:T(4,128)}, u32[]{:S(2)}) copy-start(f32[1,4,64]{2,1,0:T(4,128)} %param.15) | copy-start | bytes 3076
  108.2 39.1 %all-to-all-start.1 = ((f32[8,1,512]{2,1,0:T(1,128)}), f32[8,1,512]{2,1,0:T(1,128)S(1)}, u32[]{:S(2)}, u32[]{:S(2)}) async-start(f32[8,1,512]{2,1,0:T(1,128)} %reshape.71), calls=%async_computation.1 | async-start | bytes 32768 | tf_op jit(solution)/shard_map/all_to_all | solution.py:76
  147.3 22.6 %all-to-all-start = ((f32[8,1,32768]{2,1,0:T(1,128)}), f32[8,1,32768]{2,1,0:T(1,128)S(1)}, u32[]{:S(2)}, u32[]{:S(2)}) async-start(f32[8,1,32768]{2,1,0:T(1,128)} %reshape.69), calls=%async_computation | async-start | bytes 2097152 | tf_op jit(solution)/shard_map/all_to_all | solution.py:78
  153.3 89.4 %reduce-scatter.2.cloned.1.call-start = ((), (), s32[]{:S(2)}) async-start(), calls=%async_computation.6 | async-start | bytes 1179648 | tf_op jit(solution)/shard_map/reduce_scatter | solution.py:97
Sparse Core Ops, SparseCore 0:
  8.9 37.1 all-gather.2
  47.7 34.4 all-gather.4
  180.2 62.5 reduce-scatter.1
where the time goes:
time: 252 us; the launch traced here: 251 us
  waiting for transfers between devices  78.9 us (31%)
  blocking collectives  64.8 us (26%)
  other arithmetic  30 us (12%)
  local copies, waits for them, and re-layouts  25.7 us (10%)
  matrix products  19.8 us (8%)
  starting transfers between devices  17.6 us (7%)
  between operations  14 us (6%)
    reduce_scatter x1, waiting for transfers between devices, per_device(): lax.psum_scatter(partial_terms, 'seg', scatter_dimension=1, tiled=True)  62.7 us
    all_gather x1, blocking collectives, per_device(): gathered = lax.all_gather(decoder_rows, 'seg', axis=1, tiled=True)  33.2 us
    all_gather x1, blocking collectives, per_device(): queries = lax.all_gather(query_own, 'seg', axis=1, tiled=True)  31.6 us
    unnamed x19, local copies, waits for them, and re-layouts  21.5 us
    unnamed x3, other arithmetic  20.7 us
    all_to_all x1, waiting for transfers between devices, per_device(): lax.all_to_all(outputs[None], 'seg', split_axis=2, concat_axis=0, tiled=T...  14.8 us
    dot_general x1, matrix products, one_doc(): jnp.einsum('qhk,khd->qhd', scaled, split_values, preferred_element_type=j...  8.51 us
    all_to_all x1, starting transfers between devices, per_device(): lax.all_to_all(outputs[None], 'seg', split_axis=2, concat_axis=0, tiled=T...  6 us
  transfers between devices with their start and end apart: 6, of which 2 were waited for; matrix products, arithmetic and copies ran while one was open for 28% of the time, Pallas kernels for 0%

commit v1 on v0

--- a/solution.py
+++ b/solution.py
@@ -2,6 +2,13 @@
 import jax.numpy as jnp
 from jax import lax
 from jax.sharding import PartitionSpec as P
+
+
+def stacked_exchange(shard, axis, split, join):
+    size = lax.axis_size(axis)
+    blocks = jnp.stack(jnp.split(shard, size, axis=split), axis=0)
+    blocks = lax.all_to_all(blocks, axis, split_axis=0, concat_axis=0)
+    return jnp.concatenate(blocks, axis=join)
 
 
 def per_device(
@@ -75,7 +82,7 @@
     received = (
         lax.all_to_all(peaks[None], "seg", split_axis=2, concat_axis=0, tiled=True),
         lax.all_to_all(totals[None], "seg", split_axis=2, concat_axis=0, tiled=True),
-        lax.all_to_all(outputs[None], "seg", split_axis=2, concat_axis=0, tiled=True),
+        stacked_exchange(outputs[None], "seg", 2, 0),
     )
     peak_all, total_all, out_all = received
     largest = jnp.max(peak_all, axis=0)

time: 252 us -> 233 us (0.925)
  other arithmetic: 30 us -> 10.7 us
  waiting for transfers between devices: 78.9 us -> 84.4 us
  matrix products: 19.8 us -> 15.5 us
    unnamed x3 -> x2, other arithmetic: 20.7 us -> 1.39 us
    all_to_all x1, waiting for transfers between devices: 0.01 us -> 6.02 us  [per_device(): lax.all_to_all(peaks[None], 'seg', split_axis=2, concat_axis=0, tiled=True)]
    dot_general x1, matrix products: 8.51 us -> 3.89 us  [one_doc(): jnp.einsum('qhk,khd->qhd', scaled, split_values, preferred_element_type=j...]
    all_to_all x1 -> x0, other arithmetic: 3.1 us -> none  [per_device(): lax.all_to_all(outputs[None], 'seg', split_axis=2, concat_axis=0, tiled=T...]
    transpose x0 -> x1, local copies, waits for them, and re-layouts: none -> 2.81 us  [one_doc(): jnp.einsum('qhk,khd->qhd', scaled, split_values, preferred_element_type=j...]
    unnamed x19 -> x24, local copies, waits for them, and re-layouts: 21.5 us -> 19.8 us
  transfers between devices with their start and end apart: 6 -> 6, of which waited for: 2 -> 4; matrix products, arithmetic and copies ran while one was open for 28% -> 21% of each run, Pallas kernels for 0% -> 0%
where the time goes in v1:
time: 233 us; the launch traced here: 232 us
  waiting for transfers between devices  84.4 us (36%)
  blocking collectives  64.4 us (28%)
  local copies, waits for them, and re-layouts  27.7 us (12%)
  starting transfers between devices  15.5 us (7%)
  matrix products  15.5 us (7%)
  between operations  14 us (6%)
  other arithmetic  10.7 us (5%)
    reduce_scatter x1, waiting for transfers between devices, per_device(): lax.psum_scatter(partial_terms, 'seg', scatter_dimension=1, tiled=True)  63.1 us
    all_gather x1, blocking collectives, per_device(): gathered = lax.all_gather(decoder_rows, 'seg', axis=1, tiled=True)  33.2 us
    all_gather x1, blocking collectives, per_device(): queries = lax.all_gather(query_own, 'seg', axis=1, tiled=True)  31.2 us
    unnamed x24, local copies, waits for them, and re-layouts  19.8 us
    all_to_all x1, waiting for transfers between devices, stacked_exchange(): blocks = lax.all_to_all(blocks, axis, split_axis=0, concat_axis=0)  13.2 us
    all_to_all x1, waiting for transfers between devices, per_device(): lax.all_to_all(peaks[None], 'seg', split_axis=2, concat_axis=0, tiled=True)  6.02 us
    all_to_all x1, starting transfers between devices, per_device(): lax.all_to_all(totals[None], 'seg', split_axis=2, concat_axis=0, tiled=True)  5.74 us
    all_to_all x1, starting transfers between devices, per_device(): lax.all_to_all(peaks[None], 'seg', split_axis=2, concat_axis=0, tiled=True)  5.4 us
  transfers between devices with their start and end apart: 6, of which 4 were waited for; matrix products, arithmetic and copies ran while one was open for 21% of the time, Pallas kernels for 0%

profile of v1, /device:TPU:0, one launch (start us, length us, event | category | flops | bytes accessed | tf_op | source)
XLA Modules:
  0.0 232.2 jit_solution(5794483273872354023)
XLA Ops:
  6.5 0.0 all-gather.3.cloned.1.call-start
  6.5 0.7 all-gather.3.cloned.1.call-update
  7.3 0.0 all-gather.5.cloned.1.call-start
  7.3 0.7 all-gather.5.cloned.1.call-update
  8.0 33.2 %all_gather.12 = bf16[64,4096]{1,0:T(8,128)(2,1)S(1)} all-gather(bf16[64,512]{1,0:T(8,128)(2,1)} %param.9), channel_id=1, replica_groups=mesh['seg'=8,'rep'=4] {'seg'}, dimensions={1}, use_global_device_ids=true | all-gather | bytes 589824 | tf_op jit(solution)/shard_map/all_gather | solution.py:25
  41.3 0.2 fusion.12
  41.5 0.8 copy.27
  42.3 0.1 broadcast_in_dim.60
  43.1 0.0 copy-start.3
  43.1 0.0 copy-start.2
  43.1 6.6 %copy.25 = bf16[1,512,4096]{1,2,0:T(8,128)(2,1)} copy(bf16[1,512,4096]{2,1,0:T(8,128)(2,1)} %param.12) | data formatting | bytes 8388608 | tf_op args[3]
  49.6 6.5 %copy.30 = bf16[1,512,4096]{1,2,0:T(8,128)(2,1)} copy(bf16[1,512,4096]{2,1,0:T(8,128)(2,1)} %param.14) | data formatting | bytes 8388608 | tf_op args[5]
  56.2 0.0 copy-done.3
  56.2 0.1 copy.29
  56.3 0.1 broadcast_in_dim.63
  56.4 0.0 all-gather.3.cloned.1.call-done
  56.5 0.0 copy-done.2
  56.5 3.3 %convolution_convert_fusion = bf16[64,512]{1,0:T(8,128)(2,1)S(1)} fusion(bf16[4096,512]{1,0:T(8,128)(2,1)} %all-gather.3.cloned.1.call-done, bf16[64,4096]{1,0:T(8,128)(2,1)S(1)} %all_gather.12, f32[4096]{0:T(1024)S(1)} %copy-done.2, f32[64]{0:T(128)S(1)} %add_rsqrt_fusion), kind=kOutput, calls=%fused_computation.18 | convolution fusion | flops 269516800 | bytes 4800768 | tf_op jit(solution)/shard_map/dot_general | solution.py:29
  59.8 31.2 %all_gather.14 = bf16[64,4096]{1,0:T(8,128)(2,1)S(1)} all-gather(bf16[64,512]{1,0:T(8,128)(2,1)S(1)} %convolution_convert_fusion), channel_id=1, replica_groups=mesh['seg'=8,'rep'=4] {'seg'}, dimensions={1}, use_global_device_ids=true | all-gather | bytes 589824 | tf_op jit(solution)/shard_map/all_gather | solution.py:34
  91.0 1.1 reshape.62
  92.1 0.0 copy-start.1
  92.1 4.3 %bitcast_reduce_fusion = (f32[64,64]{0,1:T(8,128)S(1)}, f32[64,64,512]{2,1,0:T(8,128)S(1)}) fusion(f32[64,512]{1,0:T(8,128)S(1)} %bitcast.96, pred[512]{0:T(512)(128)(4,1)S(1)} %add_compare_fusion, bf16[512,64,64]{0,2,1:T(8,128)(2,1)} %bitcast.94, bf16[64,64,64]{2,1,0:T(8,128)(2,1)S(1)} %reshape.62), kind=kOutput, calls=%fused_computation.1 | convolution fusion | flops 274722816 | bytes 13255168 | tf_op jit(solution)/shard_map/while/body/eval_jaxpr/qhd,khd->qhk/dot_general | solution.py:56
  96.4 0.0 copy-done.1
  96.4 3.9 %fusion.11 = f32[64,64,64]{2,0,1:T(8,128)} fusion(bf16[512,64,64]{0,2,1:T(8,128)(2,1)S(1)} %bitcast.95, f32[64,64,512]{2,1,0:T(8,128)S(1)} %get-tuple-element.28, f32[64,512]{1,0:T(8,128)S(1)} %bitcast.105, f32[64,64]{0,1:T(8,128)S(1)} %get-tuple-element.27, f32[64,512]{1,0:T(8,128)S(1)} %bitcast.97, pred[512]{0:T(512)(128)(4,1)S(1)} %add_compare_fusion), kind=kOutput, calls=%fused_computation.15 | convolution fusion | flops 281018368 | bytes 13910528 | tf_op jit(solution)/shard_map/while/body/eval_jaxpr/qhk,khd->qhd/dot_general | solution.py:68
  100.3 0.0 copy-done
  100.3 2.8 %copy.31 = f32[64,64,64]{2,1,0:T(8,128)S(1)} copy(f32[64,64,64]{2,0,1:T(8,128)} %fusion.11) | data formatting | bytes 2097152 | tf_op jit(solution)/shard_map/while/body/eval_jaxpr/qhk,khd->qhd/transpose | solution.py:68
  103.2 0.7 broadcast_in_dim.64
  103.8 4.8 %fusion.2 = f32[64,64]{0,1:T(8,128)S(1)} fusion(f32[64,64,512]{2,1,0:T(8,128)} %copy-done, f32[64,64]{0,1:T(8,128)S(1)} %get-tuple-element.27, f32[64,512]{1,0:T(8,128)S(1)} %bitcast.98, pred[512]{0:T(512)(128)(4,1)S(1)} %add_compare_fusion), kind=kLoop, calls=%fused_computation.6 | loop fusion | flops 10481664 | bytes 8552960 | tf_op jit(solution)/shard_map/while/body/eval_jaxpr/reduce_sum | solution.py:66
  108.6 0.5 broadcast.37
  109.1 0.7 reduce.2
  109.8 0.7 reshape.69
  110.5 5.7 %all-to-all-start.2 = ((f32[8,1,512]{2,1,0:T(1,128)}), f32[8,1,512]{2,1,0:T(1,128)S(1)}, u32[]{:S(2)}, u32[]{:S(2)}) async-start(f32[8,1,512]{2,1,0:T(1,128)} %reshape.69), calls=%async_computation.2 | async-start | bytes 32768 | tf_op jit(solution)/shard_map/all_to_all | solution.py:84
  116.2 0.7 fusion.27
  116.9 0.7 fusion.26
  117.5 0.7 fusion.25
  118.2 0.7 fusion.24
  118.9 0.7 fusion.23
  119.5 0.7 fusion.22
  120.2 0.6 fusion.21
  120.8 0.7 reduce.4
  121.5 0.7 reshape.67
  122.2 0.6 all-to-all-done.2
  122.8 5.4 %all-to-all-start.1 = ((f32[8,1,512]{2,1,0:T(1,128)}), f32[8,1,512]{2,1,0:T(1,128)S(1)}, u32[]{:S(2)}, u32[]{:S(2)}) async-start(f32[8,1,512]{2,1,0:T(1,128)} %reshape.67), calls=%async_computation.1 | async-start | bytes 32768 | tf_op jit(solution)/shard_map/all_to_all | solution.py:83
  128.2 0.7 fusion.20
  128.9 6.0 %all-to-all-done.1 = f32[8,1,512]{2,1,0:T(1,128)S(1)} async-done(((f32[8,1,512]{2,1,0:T(1,128)}), f32[8,1,512]{2,1,0:T(1,128)S(1)}, u32[]{:S(2)}, u32[]{:S(2)}) %all-to-all-start.1) | async-done | bytes 16416 | tf_op jit(solution)/shard_map/all_to_all | solution.py:83
  134.9 4.2 %all-to-all-start = ((f32[8,1,64,512]{3,2,1,0:T(8,128)}), f32[8,1,64,512]{3,2,1,0:T(8,128)}, u32[]{:S(2)}, u32[]{:S(2)}) async-start(f32[8,1,64,512]{3,2,1,0:T(8,128)} %fusion.20), calls=%async_computation | async-start | bytes 2097152 | tf_op jit(solution)/shard_map/all_to_all | solution.py:10
  139.1 0.0 reduce-scatter.2.cloned.1.call-start
  139.2 0.7 reduce.3
  139.8 0.1 reshape.70
  139.9 0.7 reduce.5
  140.6 0.1 reshape.68
  140.7 0.1 copy.32
  140.9 0.6 mul.71
  141.5 0.5 mul.72
  142.0 0.1 copy.33
  142.1 0.1 div.19
  142.2 0.1 div.20
  142.3 13.2 %all-to-all-done = f32[8,1,64,512]{3,2,1,0:T(8,128)} async-done(((f32[8,1,64,512]{3,2,1,0:T(8,128)}), f32[8,1,64,512]{3,2,1,0:T(8,128)}, u32[]{:S(2)}, u32[]{:S(2)}) %all-to-all-start) | async-done | bytes 1048608 | tf_op jit(solution)/shard_map/all_to_all | solution.py:10
  155.5 1.4 multiply_reduce_fusion
  157.0 0.0 all-gather.5.cloned.1.call-done
  157.0 4.0 %fusion.28 = f32[64,4096]{1,0:T(8,128)} fusion(bf16[512,4096]{1,0:T(8,128)(2,1)} %all-gather.5.cloned.1.call-done, f32[64,512]{1,0:T(8,128)S(1)} %multiply_reduce_fusion, f32[64,512]{1,0:T(8,128)S(1)} %div.20), kind=kOutput, calls=%fused_computation.46 | convolution fusion | flops 268500992 | bytes 5505024 | tf_op jit(solution)/shard_map/dot_general | solution.py:99
  161.0 0.0 reduce-scatter.2.cloned.1.call-update
  161.0 63.1 %reduce-scatter.2.cloned.1.call-done = f32[64,512]{1,0:T(8,128)} async-done(((f32[64,4096]{1,0:T(8,128)}), f32[64,512]{1,0:T(8,128)}) %reduce-scatter.2.cloned.1.call-update) | async-done | bytes 131088 | tf_op jit(solution)/shard_map/reduce_scatter | solution.py:104
  224.2 1.5 convert_element_type.24
  (7 shorter events, 0.1 us)
Async XLA Ops:
  6.5 49.9 %all-gather.3.cloned.1.call-start = ((), (), s32[]{:S(2)}) async-start(), calls=%async_computation.4 | async-start | bytes 5242880 | tf_op jit(solution)/shard_map/all_gather | solution.py:31
  7.3 149.7 %all-gather.5.cloned.1.call-start = ((), (), s32[]{:S(2)}) async-start(), calls=%async_computation.5 | async-start | bytes 5242880 | tf_op jit(solution)/shard_map/all_gather | solution.py:101
  43.1 13.1 %copy-start.3 = (f32[1,4,64]{2,1,0:T(4,128)S(1)}, f32[1,4,64]{2,1,0:T(4,128)}, u32[]{:S(2)}) copy-start(f32[1,4,64]{2,1,0:T(4,128)} %param.15) | copy-start | bytes 3076
  43.1 13.4 %copy-start.2 = (f32[4096]{0:T(1024)S(1)}, f32[4096]{0:T(1024)}, u32[]{:S(2)}) copy-start(f32[4096]{0:T(1024)} %param.10) | copy-start | bytes 49156
  92.1 4.4 %copy-start.1 = (bf16[1,512,4096]{1,2,0:T(8,128)(2,1)S(1)}, bf16[1,512,4096]{1,2,0:T(8,128)(2,1)}, u32[]{:S(2)}) copy-start(bf16[1,512,4096]{1,2,0:T(8,128)(2,1)} %copy.30) | copy-start | bytes 12582916
  96.4 3.9 %copy-start = (f32[64,64,512]{2,1,0:T(8,128)}, f32[64,64,512]{2,1,0:T(8,128)S(1)}, u32[]{:S(2)}) copy-start(f32[64,64,512]{2,1,0:T(8,128)S(1)} %get-tuple-element.28) | copy-start | bytes 25165828
  110.5 12.3 %all-to-all-start.2 = ((f32[8,1,512]{2,1,0:T(1,128)}), f32[8,1,512]{2,1,0:T(1,128)S(1)}, u32[]{:S(2)}, u32[]{:S(2)}) async-start(f32[8,1,512]{2,1,0:T(1,128)} %reshape.69), calls=%async_computation.2 | async-start | bytes 32768 | tf_op jit(solution)/shard_map/all_to_all | solution.py:84
  122.8 12.1 %all-to-all-start.1 = ((f32[8,1,512]{2,1,0:T(1,128)}), f32[8,1,512]{2,1,0:T(1,128)S(1)}, u32[]{:S(2)}, u32[]{:S(2)}) async-start(f32[8,1,512]{2,1,0:T(1,128)} %reshape.67), calls=%async_computation.1 | async-start | bytes 32768 | tf_op jit(solution)/shard_map/all_to_all | solution.py:83
  134.9 20.6 %all-to-all-start = ((f32[8,1,64,512]{3,2,1,0:T(8,128)}), f32[8,1,64,512]{3,2,1,0:T(8,128)}, u32[]{:S(2)}, u32[]{:S(2)}) async-start(f32[8,1,64,512]{3,2,1,0:T(8,128)} %fusion.20), calls=%async_computation | async-start | bytes 2097152 | tf_op jit(solution)/shard_map/all_to_all | solution.py:10
  139.1 85.0 %reduce-scatter.2.cloned.1.call-start = ((), (), s32[]{:S(2)}) async-start(), calls=%async_computation.6 | async-start | bytes 1179648 | tf_op jit(solution)/shard_map/reduce_scatter | solution.py:104
Sparse Core Ops, SparseCore 0:
  8.9 37.1 all-gather.2
  47.7 34.4 all-gather.4
  161.1 62.9 reduce-scatter.1
